TPU v7x, 512 devices: a whole 4x4x16 slice. The times are simulated.
512 devices in a mesh: dp: 64 (over x, z_lo, core), mp: 8 (over y, z_hi).
Axes of the slice: x: 4, y: 4, z: 16 (z_hi: 2, z_lo: 8; z = z_hi * 8 + z_lo), core: 2. Of those that a mesh axis runs over, the one named last changes fastest.
Arguments:
- states: bfloat16 [128, 64, 2048], P('dp', None, 'mp'), may hold values from -6 to 6
- w_qkv: bfloat16 [3, 2048, 2048], P(None, 'dp', 'mp'), may hold values from -0.125 to 0.125
- w_out: bfloat16 [2048, 2048], P('dp', 'mp'), may hold values from -0.125 to 0.125
- cache_keys: bfloat16 [128, 384, 2048], P('dp', None, 'mp'), as said below
- cache_values: bfloat16 [128, 384, 2048], P('dp', None, 'mp'), may hold values from -6 to 6
- parents: int32 [128, 64], P('dp'), may hold values from 0 to 62, as said below
- accept: int32 [128, 8], P('dp'), may hold values from 0 to 63, as said below
- lengths: int32 [128], replicated, may hold values from 48 to 384
- perm: int32 [128], replicated, may hold values from 0 to 127, each once
Outputs:
- tree_out: bfloat16 [128, 64, 2048], P('dp', None, 'mp')
- new_keys: bfloat16 [128, 8, 2048], P('dp', None, 'mp')
- new_values: bfloat16 [128, 8, 2048], P('dp', None, 'mp')
Inputs may be any that keep to these rules, and one draw needn't show every extreme that they name: parents[r, 0] = 0 for the root and parents[r, i] < i for every other node. `accept`: each row is a chain of 8 nodes from the root (node 0) downward, each entry the parent of the next. `perm`: each request stands in exactly one slot. `cache_keys`: keys of earlier positions, already rotated; slots at or past the request's length hold arbitrary values.
All inputs are finite; a program needn't handle non-finite values.
Results may differ from a plain program's by a relative error of at most 0.012.
The roundings to bfloat16 on the way count: a program that leaves them out, or rounds other values in their place, can miss the bound.
Values may be sent and summed in bfloat16 or wider, within the bound.
A program may use at most 64 MiB of HBM per device.

v0:
```python
import jax
import jax.numpy as jnp
from jax import lax
from jax.sharding import PartitionSpec as P

HEAD_DIM = 128
EPSILON = 1e-05
ROPE_BASE = 10000.0
NEG_FILL = -1e30


def layer_norm(rows):
    mean_val = jnp.mean(rows, axis=-1, keepdims=True)
    centred = rows - mean_val
    variance = jnp.mean(centred * centred, axis=-1, keepdims=True)
    return centred * lax.rsqrt(variance + EPSILON)


def rotate(values, position):
    half = values.shape[-1] // 2
    freqs = ROPE_BASE ** (-(jnp.arange(half, dtype=jnp.float32) * 2.0 / values.shape[-1]))
    angle = position[:, :, None, None] * freqs
    cosine = jnp.cos(angle)
    sine = jnp.sin(angle)
    first = values[..., :half]
    second = values[..., half:]
    return jnp.concatenate(
        [first * cosine - second * sine, second * cosine + first * sine], axis=-1
    )


def closure(parents):
    tree_len = parents.shape[-1]
    node_ids = jnp.arange(tree_len, dtype=jnp.int32)
    linked = (parents[:, :, None] == node_ids[None, None, :]) & (node_ids[None, :, None] > 0)
    reach = jnp.eye(tree_len, dtype=jnp.float32)[None] + linked.astype(jnp.float32)
    covered = 1
    while covered < tree_len:
        reach = jnp.minimum(jnp.einsum("rij,rjk->rik", reach, reach), 1.0)
        covered = covered * 2
    return reach


def local(states, w_qkv, w_out, cache_keys, cache_values, parents, accept, lengths, perm):
    req_count, tree_len, local_dim = states.shape
    cache_len = cache_keys.shape[1]
    heads_here = local_dim // HEAD_DIM
    scale = HEAD_DIM ** (-0.5)
    flat_rows = req_count * tree_len
    gathered = lax.all_gather(states, "mp", axis=2, tiled=True)
    normed = layer_norm(gathered.astype(jnp.float32)).astype(jnp.bfloat16).reshape(flat_rows, -1)

    def add_one(piece):
        return jnp.dot(normed, piece, preferred_element_type=jnp.float32)

    query_flat = add_one(lax.all_gather(w_qkv[0], "dp", axis=0, tiled=True))
    key_flat = add_one(lax.all_gather(w_qkv[1], "dp", axis=0, tiled=True))
    value_flat = add_one(lax.all_gather(w_qkv[2], "dp", axis=0, tiled=True))
    dealt_ids = lax.dynamic_slice_in_dim(perm, lax.axis_index("dp") * req_count, req_count)
    matches = dealt_ids[:, None] == jnp.arange(perm.shape[0], dtype=jnp.int32)[None, :]
    own_lengths = jnp.sum(jnp.where(matches, lengths[None, :], 0), axis=1)
    reach = closure(parents)
    depth = jnp.sum(reach, axis=-1) - 1.0
    position = own_lengths.astype(jnp.float32)[:, None] + depth
    shape_heads = (req_count, tree_len, heads_here, HEAD_DIM)
    queries = rotate(query_flat.reshape(shape_heads), position).astype(jnp.bfloat16)
    keys_new = rotate(key_flat.reshape(shape_heads), position).astype(jnp.bfloat16)
    values_new = value_flat.reshape(shape_heads).astype(jnp.bfloat16)
    keys_old = cache_keys.reshape(req_count, cache_len, heads_here, HEAD_DIM)
    values_old = cache_values.reshape(req_count, cache_len, heads_here, HEAD_DIM)
    tree_scores = (
        jnp.einsum("rthd,rshd->rhts", queries, keys_new, preferred_element_type=jnp.float32) * scale
    )
    tree_scores = jnp.where(reach[:, None] > 0, tree_scores, NEG_FILL)
    cache_scores = (
        jnp.einsum("rthd,rchd->rhtc", queries, keys_old, preferred_element_type=jnp.float32) * scale
    )
    valid = jnp.arange(cache_len, dtype=jnp.int32)[None, :] < own_lengths[:, None]
    cache_scores = jnp.where(valid[:, None, None, :], cache_scores, NEG_FILL)
    peak = jnp.maximum(jnp.max(cache_scores, axis=-1), jnp.max(tree_scores, axis=-1))
    cache_exp = jnp.exp(cache_scores - peak[..., None])
    tree_exp = jnp.exp(tree_scores - peak[..., None])
    denom = jnp.sum(cache_exp, axis=-1) + jnp.sum(tree_exp, axis=-1)
    cache_prob = (cache_exp / denom[..., None]).astype(jnp.bfloat16)
    tree_prob = (tree_exp / denom[..., None]).astype(jnp.bfloat16)
    mixed = jnp.einsum(
        "rhtc,rchd->rthd", cache_prob, values_old, preferred_element_type=jnp.float32
    )
    mixed = mixed + jnp.einsum(
        "rhts,rshd->rthd", tree_prob, values_new, preferred_element_type=jnp.float32
    )
    attended = mixed.astype(jnp.bfloat16).reshape(flat_rows, local_dim)
    heads_all = lax.all_gather(attended, "mp", axis=1, tiled=True)
    projected_out = jnp.dot(
        heads_all,
        lax.all_gather(w_out, "dp", axis=0, tiled=True),
        preferred_element_type=jnp.float32,
    )
    tree_out = (
        states.astype(jnp.float32) + projected_out.reshape(req_count, tree_len, local_dim)
    ).astype(jnp.bfloat16)
    picker = (accept[:, :, None] == jnp.arange(tree_len, dtype=jnp.int32)[None, None, :]).astype(
        jnp.bfloat16
    )
    stacked = jnp.concatenate(
        [
            keys_new.reshape(req_count, tree_len, local_dim),
            values_new.reshape(req_count, tree_len, local_dim),
        ],
        axis=-1,
    )
    chosen = jnp.einsum("rdt,rtn->rdn", picker, stacked, preferred_element_type=jnp.float32).astype(
        jnp.bfloat16
    )
    return (tree_out, chosen[..., :local_dim], chosen[..., local_dim:])


def solution(mesh):
    in_specs = (
        P("dp", None, "mp"),
        P(None, "dp", "mp"),
        P("dp", "mp"),
        P("dp", None, "mp"),
        P("dp", None, "mp"),
        P("dp", None),
        P("dp", None),
        P(),
        P(),
    )
    out_specs = (P("dp", None, "mp"), P("dp", None, "mp"), P("dp", None, "mp"))
    return jax.shard_map(local, mesh=mesh, in_specs=in_specs, out_specs=out_specs, check_vma=False)
```

profile of v0, /device:TPU:33, one launch (start us, length us, event | category | flops | bytes accessed | tf_op | source)
XLA Modules:
  0.0 533.2 jit_solution(12800749686257656289)
XLA Ops:
  7.2 0.0 copy-start
  7.2 0.0 all-gather.14.cloned.1.call-start
  7.2 1.4 fusion.52
  8.6 0.0 copy-start.2
  8.6 0.0 all-gather.14.cloned.1.call-update
  8.7 0.0 all-gather.10.cloned.1.call-start
  8.7 0.7 all-gather.10.cloned.1.call-update
  9.4 0.0 all-gather.12.cloned.1.call-start
  9.5 0.7 all-gather.12.cloned.1.call-update
  10.1 0.0 all-gather.8.cloned.1.call-start
  10.2 0.5 all-gather.8.cloned.1.call-update
  10.8 0.0 copy-start.6
  10.8 0.6 copy-done.6
  11.4 0.0 copy-start.7
  11.4 0.1 dynamic_slice.3
  11.5 0.6 copy-done.7
  12.1 0.2 fusion.45
  12.3 0.1 iota_compare_fusion.4
  12.3 0.0 copy-done.2
  12.3 83.0 %all_gather.18 = bf16[2,64,2048]{2,1,0:T(8,128)(2,1)S(1)} all-gather(bf16[2,64,256]{2,1,0:T(8,128)(2,1)S(1)} %copy-done.2), channel_id=1, replica_groups=mesh['dp'=64,'mp'=8] {'mp'}, dimensions={2}, use_global_device_ids=true | all-gather | bytes 589824 | tf_op jit(solution)/shard_map/all_gather | solution.py:50
  95.3 0.2 convert_reduce_fusion
  95.5 0.3 fusion.6
  95.8 0.0 copy-start.4
  95.8 0.7 copy-done.4
  96.5 0.4 convolution_minimum_fusion.4
  96.9 0.3 convolution_minimum_fusion.2
  97.2 0.4 fusion.54
  97.5 0.1 copy.33
  97.7 0.1 add_add_fusion
  97.7 0.3 multiply_cosine_fusion
  98.0 50.2 %all-gather.14.cloned.1.call-done = bf16[1,2048,256]{2,1,0:T(8,128)(2,1)} async-done(((bf16[1,32,256]{2,1,0:T(8,128)(2,1)}), bf16[1,2048,256]{2,1,0:T(8,128)(2,1)}) %all-gather.14.cloned.1.call-update) | async-done | bytes 1048592 | tf_op jit(solution)/shard_map/all_gather | solution.py:58
  148.3 1.5 copy.36
  149.7 122.3 %all-gather.10.cloned.1.call-done = bf16[1,2048,256]{2,1,0:T(8,128)(2,1)} async-done(((bf16[1,32,256]{2,1,0:T(8,128)(2,1)}), bf16[1,2048,256]{2,1,0:T(8,128)(2,1)}) %all-gather.10.cloned.1.call-update) | async-done | bytes 1048592 | tf_op jit(solution)/shard_map/all_gather | solution.py:56
  272.0 1.5 copy.29
  273.5 116.4 %all-gather.12.cloned.1.call-done = bf16[1,2048,256]{2,1,0:T(8,128)(2,1)} async-done(((bf16[1,32,256]{2,1,0:T(8,128)(2,1)}), bf16[1,2048,256]{2,1,0:T(8,128)(2,1)}) %all-gather.12.cloned.1.call-update) | async-done | bytes 1048592 | tf_op jit(solution)/shard_map/all_gather | solution.py:57
  389.9 2.3 copy.34
  392.2 0.0 copy-start.1
  392.2 0.5 fusion.42
  392.7 0.7 copy-done.1
  393.4 0.5 fusion.40
  393.9 0.1 subtract_convert_fusion
  394.0 0.1 multiply_subtract_fusion
  394.2 0.3 fusion.56
  394.4 0.0 copy-done
  394.4 0.4 fusion.55
  394.9 0.2 fusion.13
  395.1 0.5 convolution_convert_fusion
  395.6 0.0 copy-start.3
  395.6 0.2 convolution_bitcast_fusion.1
  395.9 0.8 copy-done.3
  396.6 0.3 fusion.5
  396.9 0.1 copy.38
  397.0 0.1 copy_bitcast_fusion.1
  397.1 66.5 %all_gather.22 = bf16[128,2048]{1,0:T(8,128)(2,1)S(1)} all-gather(bf16[128,256]{1,0:T(8,128)(2,1)S(1)} %bitcast.82), channel_id=1, replica_groups=mesh['dp'=64,'mp'=8] {'mp'}, dimensions={1}, use_global_device_ids=true | all-gather | bytes 589824 | tf_op jit(solution)/shard_map/all_gather | solution.py:93
  463.6 59.5 %all-gather.8.cloned.1.call-done = bf16[2048,256]{1,0:T(8,128)(2,1)} async-done(((bf16[32,256]{1,0:T(8,128)(2,1)}), bf16[2048,256]{1,0:T(8,128)(2,1)}) %all-gather.8.cloned.1.call-update) | async-done | bytes 1048592 | tf_op jit(solution)/shard_map/all_gather | solution.py:96
  523.0 1.5 fusion.58
  524.6 0.6 add_convert_fusion
  525.2 0.0 copy-start.5
  525.2 0.7 copy-done.5
  525.9 0.2 convolution_convert_fusion.1
  526.1 0.6 fusion.53
  (11 shorter events, 0.1 us)
Async XLA Ops:
  7.2 387.3 %copy-start = (bf16[2,384,256]{2,1,0:T(8,128)(2,1)S(1)}, bf16[2,384,256]{2,1,0:T(8,128)(2,1)}, u32[]{:S(2)}) copy-start(bf16[2,384,256]{2,1,0:T(8,128)(2,1)} %param.12) | copy-start | bytes 1179652
  7.2 141.1 %all-gather.14.cloned.1.call-start = ((), (), s32[]{:S(2)}) async-start(), calls=%async_computation.3 | async-start | bytes 1064960 | tf_op jit(solution)/shard_map/all_gather | solution.py:58
  8.6 3.7 copy-start.2
  8.7 263.3 %all-gather.10.cloned.1.call-start = ((), (), s32[]{:S(2)}) async-start(), calls=%async_computation.1 | async-start | bytes 1064960 | tf_op jit(solution)/shard_map/all_gather | solution.py:56
  9.4 380.5 %all-gather.12.cloned.1.call-start = ((), (), s32[]{:S(2)}) async-start(), calls=%async_computation.2 | async-start | bytes 1064960 | tf_op jit(solution)/shard_map/all_gather | solution.py:57
  10.1 512.9 %all-gather.8.cloned.1.call-start = ((), (), s32[]{:S(2)}) async-start(), calls=%async_computation | async-start | bytes 1064960 | tf_op jit(solution)/shard_map/all_gather | solution.py:96
  10.8 0.7 copy-start.6
  11.4 0.7 copy-start.7
  95.8 0.7 copy-start.4
  392.2 1.2 copy-start.1
  395.6 1.0 copy-start.3
  525.2 0.7 copy-start.5
Sparse Core Ops, SparseCore 0:
  10.1 138.0 all-gather.13
  151.0 120.9 all-gather.9
  274.2 115.7 all-gather.11
  391.9 131.0 all-gather.7
where the time goes:
time: 534 us; the launch traced here: 533 us
  waiting for transfers between devices  350 us (66%)
  blocking collectives  149 us (28%)
  between operations  14 us (3%)
  local copies, waits for them, and re-layouts  11.6 us (2%)
  matrix products  5.43 us (1%)
    all_gather x1, waiting for transfers between devices, local(): query_flat = add_one(lax.all_gather(w_qkv[0], 'dp', axis=0, tiled=True))  122 us
    all_gather x1, waiting for transfers between devices, local(): key_flat = add_one(lax.all_gather(w_qkv[1], 'dp', axis=0, tiled=True))  116 us
    all_gather x1, blocking collectives, local(): gathered = lax.all_gather(states, 'mp', axis=2, tiled=True)  83 us
    all_gather x1, blocking collectives, local(): heads_all = lax.all_gather(attended, 'mp', axis=1, tiled=True)  66.5 us
    all_gather x1, waiting for transfers between devices, local(): lax.all_gather(w_out, 'dp', axis=0, tiled=True)  59.5 us
    all_gather x1, waiting for transfers between devices, local(): value_flat = add_one(lax.all_gather(w_qkv[2], 'dp', axis=0, tiled=True))  50.2 us
  transfers between devices with their start and end apart: 4, of which 4 were waited for; matrix products, arithmetic and copies ran while one was open for 2% of the time, Pallas kernels for 0%

commit v1 on v0

--- a/solution.py
+++ b/solution.py
@@ -42,6 +42,12 @@
 
 
 def local(states, w_qkv, w_out, cache_keys, cache_values, parents, accept, lengths, perm):
+
+    def wrap_the_shifts_all(obj, chip_axis):
+        a_now = jnp.stack([obj] * lax.axis_size(chip_axis))
+        x_new = lax.all_to_all(a_now, chip_axis, 0, 0)
+        return jnp.concatenate(x_new, axis=0)
+
     req_count, tree_len, local_dim = states.shape
     cache_len = cache_keys.shape[1]
     heads_here = local_dim // HEAD_DIM
@@ -54,7 +60,7 @@
         return jnp.dot(normed, piece, preferred_element_type=jnp.float32)
 
     query_flat = add_one(lax.all_gather(w_qkv[0], "dp", axis=0, tiled=True))
-    key_flat = add_one(lax.all_gather(w_qkv[1], "dp", axis=0, tiled=True))
+    key_flat = add_one(wrap_the_shifts_all(w_qkv[1], "dp"))
     value_flat = add_one(lax.all_gather(w_qkv[2], "dp", axis=0, tiled=True))
     dealt_ids = lax.dynamic_slice_in_dim(perm, lax.axis_index("dp") * req_count, req_count)
     matches = dealt_ids[:, None] == jnp.arange(perm.shape[0], dtype=jnp.int32)[None, :]

time: 534 us -> 419 us (0.78)
  the two profiles are of different devices: /device:TPU:33 before, /device:TPU:1 now
where the time goes in v1:
time: 419 us; the launch traced here: 418 us
  waiting for transfers between devices  215 us (51%)
  blocking collectives  148 us (35%)
  starting transfers between devices  17.2 us (4%)
  between operations  14.1 us (3%)
  local copies, waits for them, and re-layouts  13 us (3%)
  matrix products  8.59 us (2%)
    all_gather x1, waiting for transfers between devices, local(): query_flat = add_one(lax.all_gather(w_qkv[0], 'dp', axis=0, tiled=True))  121 us
    all_gather x1, blocking collectives, local(): heads_all = lax.all_gather(attended, 'mp', axis=1, tiled=True)  75.9 us
    all_gather x1, blocking collectives, local(): gathered = lax.all_gather(states, 'mp', axis=2, tiled=True)  72.2 us
    all_gather x1, waiting for transfers between devices, local(): value_flat = add_one(lax.all_gather(w_qkv[2], 'dp', axis=0, tiled=True))  48.2 us
    all_gather x1, waiting for transfers between devices, local(): lax.all_gather(w_out, 'dp', axis=0, tiled=True)  44.4 us
    all_to_all x1, starting transfers between devices, wrap_the_shifts_all(): x_new = lax.all_to_all(a_now, chip_axis, 0, 0)  17 us
  transfers between devices with their start and end apart: 4, of which 3 were waited for; matrix products, arithmetic and copies ran while one was open for 3% of the time, Pallas kernels for 0%

profile of v1, /device:TPU:1, one launch (start us, length us, event | category | flops | bytes accessed | tf_op | source)
XLA Modules:
  0.0 418.0 jit_solution(2629794247365147682)
XLA Ops:
  7.2 0.0 copy-start
  7.2 0.0 all-gather.10.cloned.1.call-start
  7.2 1.4 fusion.52
  8.6 0.0 all-gather.10.cloned.1.call-update
  8.7 0.0 all-gather.8.cloned.1.call-start
  8.7 0.7 all-gather.8.cloned.1.call-update
  9.4 1.1 stack.3
  10.5 17.0 %all-to-all-start = ((bf16[64,32,256]{2,1,0:T(8,128)(2,1)}), bf16[64,32,256]{2,1,0:T(8,128)(2,1)S(1)}, u32[]{:S(2)}, u32[]{:S(2)}) async-start(bf16[64,32,256]{2,1,0:T(8,128)(2,1)} %stack.3), calls=%async_computation | async-start | bytes 2097152 | tf_op jit(solution)/shard_map/all_to_all | solution.py:48
  27.6 0.0 all-gather.6.cloned.1.call-start
  27.6 0.7 all-gather.6.cloned.1.call-update
  28.3 0.0 copy-start.15
  28.3 0.6 copy-done.15
  29.0 0.1 dynamic_slice.3
  29.1 0.6 copy-done.16
  29.6 0.2 fusion.45
  29.8 0.0 copy-start.13
  29.9 0.7 copy-done.13
  30.5 0.4 convolution_minimum_fusion.4
  30.9 0.3 convolution_minimum_fusion.2
  31.2 0.4 fusion.54
  31.6 0.1 copy.33
  31.7 0.7 copy-done.5
  32.4 72.2 %all_gather.15 = bf16[2,64,2048]{2,1,0:T(8,128)(2,1)S(1)} all-gather(bf16[2,64,256]{2,1,0:T(8,128)(2,1)S(1)} %copy-done.5), channel_id=1, replica_groups=mesh['dp'=64,'mp'=8] {'mp'}, dimensions={2}, use_global_device_ids=true | all-gather | bytes 589824 | tf_op jit(solution)/shard_map/all_gather | solution.py:56
  104.6 0.2 convert_reduce_fusion
  104.8 0.3 fusion.6
  105.0 0.1 iota_compare_fusion.4
  105.1 0.1 add_add_fusion
  105.2 0.3 multiply_cosine_fusion
  105.5 0.0 copy-start.1
  105.5 0.0 copy-start.3
  105.5 48.2 %all-gather.10.cloned.1.call-done = bf16[1,2048,256]{2,1,0:T(8,128)(2,1)} async-done(((bf16[1,32,256]{2,1,0:T(8,128)(2,1)}), bf16[1,2048,256]{2,1,0:T(8,128)(2,1)}) %all-gather.10.cloned.1.call-update) | async-done | bytes 1048592 | tf_op jit(solution)/shard_map/all_gather | solution.py:64
  153.7 1.5 copy.36
  155.2 120.9 %all-gather.8.cloned.1.call-done = bf16[1,2048,256]{2,1,0:T(8,128)(2,1)} async-done(((bf16[1,32,256]{2,1,0:T(8,128)(2,1)}), bf16[1,2048,256]{2,1,0:T(8,128)(2,1)}) %all-gather.8.cloned.1.call-update) | async-done | bytes 1048592 | tf_op jit(solution)/shard_map/all_gather | solution.py:62
  276.1 2.3 copy.29
  278.3 1.7 fusion.42
  280.1 0.1 subtract_convert_fusion
  280.2 1.1 convolution_convert_fusion
  281.3 1.0 fusion.55
  282.3 0.0 all-to-all-done
  282.3 0.6 copy.34
  283.0 0.7 copy-done.10
  283.7 1.2 fusion.40
  284.9 0.0 copy-done.2
  284.9 0.0 copy-done.4
  284.9 0.1 multiply_subtract_fusion
  285.0 0.3 fusion.56
  285.3 0.0 copy-start.8
  285.3 0.7 copy-done.8
  286.0 0.0 copy-start.7
  286.0 0.0 copy-start.12
  286.0 0.2 fusion.13
  286.3 0.6 copy-done.7
  286.8 0.2 convolution_bitcast_fusion.1
  287.1 0.0 copy-done.12
  287.1 0.3 fusion.5
  287.4 0.1 copy.38
  287.5 0.1 copy_bitcast_fusion.1
  287.6 75.9 %all_gather.18 = bf16[128,2048]{1,0:T(8,128)(2,1)S(1)} all-gather(bf16[128,256]{1,0:T(8,128)(2,1)S(1)} %bitcast.84), channel_id=1, replica_groups=mesh['dp'=64,'mp'=8] {'mp'}, dimensions={1}, use_global_device_ids=true | all-gather | bytes 589824 | tf_op jit(solution)/shard_map/all_gather | solution.py:99
  363.4 44.4 %all-gather.6.cloned.1.call-done = bf16[2048,256]{1,0:T(8,128)(2,1)} async-done(((bf16[32,256]{1,0:T(8,128)(2,1)}), bf16[2048,256]{1,0:T(8,128)(2,1)}) %all-gather.6.cloned.1.call-update) | async-done | bytes 1048592 | tf_op jit(solution)/shard_map/all_gather | solution.py:102
  407.8 1.5 fusion.58
  409.3 0.6 add_convert_fusion
  410.0 0.7 copy-done.14
  410.6 0.2 convolution_convert_fusion.1
  410.8 0.6 fusion.53
  (26 shorter events, 0.1 us)
Async XLA Ops:
  7.2 274.2 %copy-start = (bf16[2,384,256]{2,1,0:T(8,128)(2,1)S(1)}, bf16[2,384,256]{2,1,0:T(8,128)(2,1)}, u32[]{:S(2)}) copy-start(bf16[2,384,256]{2,1,0:T(8,128)(2,1)} %param.12) | copy-start | bytes 1179652
  7.2 146.5 %all-gather.10.cloned.1.call-start = ((), (), s32[]{:S(2)}) async-start(), calls=%async_computation.3 | async-start | bytes 1064960 | tf_op jit(solution)/shard_map/all_gather | solution.py:64
  8.7 267.4 %all-gather.8.cloned.1.call-start = ((), (), s32[]{:S(2)}) async-start(), calls=%async_computation.2 | async-start | bytes 1064960 | tf_op jit(solution)/shard_map/all_gather | solution.py:62
  10.5 271.8 %all-to-all-start = ((bf16[64,32,256]{2,1,0:T(8,128)(2,1)}), bf16[64,32,256]{2,1,0:T(8,128)(2,1)S(1)}, u32[]{:S(2)}, u32[]{:S(2)}) async-start(bf16[64,32,256]{2,1,0:T(8,128)(2,1)} %stack.3), calls=%async_computation | async-start | bytes 2097152 | tf_op jit(solution)/shard_map/all_to_all | solution.py:48
  27.6 380.2 %all-gather.6.cloned.1.call-start = ((), (), s32[]{:S(2)}) async-start(), calls=%async_computation.1 | async-start | bytes 1064960 | tf_op jit(solution)/shard_map/all_gather | solution.py:102
  28.3 0.7 copy-start.15
  29.0 0.7 copy-start.16
  29.8 0.7 copy-start.13
  31.6 0.8 copy-start.5
  104.8 175.4 %copy-start.9 = (f32[2,64]{1,0:T(2,128)}, f32[2,64]{1,0:T(2,128)S(1)}, u32[]{:S(2)}) copy-start(f32[2,64]{1,0:T(2,128)S(1)} %broadcast_multiply_fusion) | copy-start | bytes 1540
  105.1 175.0 %copy-start.11 = (f32[2,64]{1,0:T(2,128)}, f32[2,64]{1,0:T(2,128)S(1)}, u32[]{:S(2)}) copy-start(f32[2,64]{1,0:T(2,128)S(1)} %add_rsqrt_fusion) | copy-start | bytes 1540
  105.5 174.5 %copy-start.1 = (f32[2,64,64]{2,1,0:T(8,128)}, f32[2,64,64]{2,1,0:T(8,128)S(1)}, u32[]{:S(2)}) copy-start(f32[2,64,64]{2,1,0:T(8,128)S(1)} %get-tuple-element.12) | copy-start | bytes 98308
  105.5 174.5 %copy-start.3 = (f32[2,64,64]{2,1,0:T(8,128)}, f32[2,64,64]{2,1,0:T(8,128)S(1)}, u32[]{:S(2)}) copy-start(f32[2,64,64]{2,1,0:T(8,128)S(1)} %get-tuple-element.13) | copy-start | bytes 98308
  283.0 0.7 copy-start.10
  283.7 1.2 copy-start.2
  283.7 1.2 copy-start.4
  285.3 0.7 copy-start.8
  286.0 0.8 copy-start.7
  286.0 1.0 copy-start.12
  363.4 45.9 %copy-start.6 = (bf16[2,64,256]{2,1,0:T(8,128)(2,1)S(1)}, bf16[2,64,256]{2,1,0:T(8,128)(2,1)}, u32[]{:S(2)}) copy-start(bf16[2,64,256]{2,1,0:T(8,128)(2,1)} %param.9) | copy-start | bytes 196612
  410.0 0.7 copy-start.14
Sparse Core Ops, SparseCore 0:
  10.1 143.5 all-gather.9
  156.4 119.5 all-gather.7
  278.2 129.5 all-gather.5
